TPU v7x, 512 devices: a whole 4x8x8 slice. The times are simulated.
512 devices in a mesh: rep: 4 (over z_hi), fsdp: 128 (over z_lo, y, x, core).
Axes of the slice: x: 4, y: 8, z: 8 (z_hi: 4, z_lo: 2; z = z_hi * 2 + z_lo), core: 2. Of those that a mesh axis runs over, the one named last changes fastest.
Arguments:
- hidden: bfloat16 [4, 32768, 128], P('rep', 'fsdp'), may hold values from -4 to 4
- cotangent: bfloat16 [4, 32768, 8192], P('rep', 'fsdp'), may hold values from -0.0625 to 0.0625
- master: float32 [4, 128, 8192], P('rep', 'fsdp'), may hold values from -6 to 6
- adam_m: float32 [4, 128, 8192], P('rep', 'fsdp'), may hold values from -0.3125 to 0.3125
- adam_v: float32 [4, 128, 8192], P('rep', 'fsdp'), may hold values from 0.0005 to 0.008
- anchor: float32 [128, 8192], P('fsdp'), may hold values from -6 to 6
- outer_mom: float32 [128, 8192], P('fsdp'), may hold values from -1.75 to 1.75
- next_hidden: bfloat16 [4, 4096, 128], P('rep', 'fsdp'), may hold values from -0.5 to 0.5
Outputs:
- grad_hidden: bfloat16 [4, 32768, 128], P('rep', 'fsdp')
- merged: float32 [4, 128, 8192], P('rep', 'fsdp')
- new_anchor: float32 [128, 8192], P('fsdp')
- new_momentum: float32 [128, 8192], P('fsdp')
- next_out: bfloat16 [4, 4096, 8192], P('rep', 'fsdp')
All inputs are finite; a program needn't handle non-finite values.
Results may differ from a plain program's by a relative error of at most 0.018.
Values may be sent and summed in bfloat16 or wider, within the bound.
A program may use at most 64 MiB of HBM per device.

v0:
```python
import math

import jax
import jax.numpy as jnp
from jax import lax
from jax.sharding import PartitionSpec as P

BETA_ONE = 0.9
BETA_TWO = 0.95
INNER_LR = 0.3
DECAY = 0.1
EPS = 1e-08
OUTER_LR = 0.7
MOMENTUM = 0.9
ALPHA = 0.5
STEP = 100


def hadamard_table():
    index = jnp.arange(128, dtype=jnp.int32)
    count = jnp.zeros((128, 128), jnp.int32)
    for bit in range(7):
        left = jnp.bitwise_and(jnp.right_shift(index, bit), 1)
        count = count + left[:, None] * left[None, :]
    return (1 - 2 * (count % 2)).astype(jnp.float32)


def sign_vector(width):
    index = jnp.arange(width, dtype=jnp.int32)
    return (1 - 2 * (index * 97 % 251 % 2)).astype(jnp.float32)


def block_rotate(values, table):
    rows, width = values.shape
    blocks = values.reshape(rows, width // 128, 128)
    out = jnp.einsum("rbk,kj->rbj", blocks, table, precision=lax.Precision.HIGHEST)
    return out.reshape(rows, width) * (1.0 / math.sqrt(128.0))


def shards(hidden, cotangent, master, adam_m, adam_v, anchor, outer_mom, next_hidden):
    table = hadamard_table()
    width = master.shape[2]
    hidden_rows = hidden[0]
    cotangent_rows = cotangent[0]
    weights16 = master[0].astype(jnp.bfloat16)
    all_weights = lax.all_gather(weights16, "fsdp", axis=0, tiled=True)
    grad_hidden = lax.dot_general(
        cotangent_rows, all_weights, (((1,), (1,)), ((), ())), preferred_element_type=jnp.float32
    ).astype(jnp.bfloat16)
    full_grad = lax.dot_general(
        hidden_rows, cotangent_rows, (((0,), (0,)), ((), ())), preferred_element_type=jnp.float32
    )
    gradient = lax.psum_scatter(full_grad, "fsdp", scatter_dimension=0, tiled=True)
    corr_one = 1.0 - BETA_ONE**STEP
    corr_two = 1.0 - BETA_TWO**STEP
    first = BETA_ONE * adam_m[0] + (1.0 - BETA_ONE) * gradient
    second = BETA_TWO * adam_v[0] + (1.0 - BETA_TWO) * gradient * gradient
    update = first / corr_one / (jnp.sqrt(second / corr_two) + EPS) + DECAY * master[0]
    inner = master[0] - INNER_LR * update
    signs = sign_vector(width)
    rotated = block_rotate((anchor - inner) * signs[None, :], table).astype(jnp.bfloat16)
    replicas = lax.axis_size("rep")
    total = lax.psum(rotated.astype(jnp.float32).astype(jnp.bfloat16), "rep").astype(jnp.float32)
    mean_delta = block_rotate(total, table) * signs[None, :] / replicas
    new_momentum = MOMENTUM * outer_mom + mean_delta
    new_anchor = anchor - OUTER_LR * (MOMENTUM * new_momentum + mean_delta)
    merged = ALPHA * inner + (1.0 - ALPHA) * new_anchor
    merged16 = merged.astype(jnp.bfloat16)
    next_rows = next_hidden[0]
    all_merged = lax.all_gather(merged16, "fsdp", axis=0, tiled=True)
    next_out = jnp.dot(next_rows, all_merged, preferred_element_type=jnp.float32).astype(
        jnp.bfloat16
    )
    return (grad_hidden[None], merged[None], new_anchor, new_momentum, next_out[None])


def solution(mesh):
    in_specs = (
        P("rep", "fsdp", None),
        P("rep", "fsdp", None),
        P("rep", "fsdp", None),
        P("rep", "fsdp", None),
        P("rep", "fsdp", None),
        P("fsdp", None),
        P("fsdp", None),
        P("rep", "fsdp", None),
    )
    out_specs = (
        P("rep", "fsdp", None),
        P("rep", "fsdp", None),
        P("fsdp", None),
        P("fsdp", None),
        P("rep", "fsdp", None),
    )
    return jax.shard_map(shards, mesh=mesh, in_specs=in_specs, out_specs=out_specs, check_vma=False)
```

profile of v0, /device:TPU:1, one launch (start us, length us, event | category | flops | bytes accessed | tf_op | source)
XLA Modules:
  0.0 1569.0 jit_solution(18300237138548457707)
XLA Ops:
  7.2 0.0 copy-start
  7.2 0.0 all-reduce.3.cloned.1.call-start
  7.2 0.8 copy-done
  8.0 4.9 fusion.1
  12.9 0.0 copy-start.6
  12.9 0.0 all-reduce.3.cloned.1.call-update
  13.0 0.0 all-gather.5.cloned.1.call-start
  13.0 0.7 copy-done.3
  13.7 0.6 fusion.32
  14.3 0.0 all-gather.5.cloned.1.call-update
  14.3 0.0 all-gather.7.cloned.1.call-start
  14.4 1.3 dynamic-slice
  15.7 1102.8 %all-reduce.3.cloned.1.call-done = f32[128,8192]{1,0:T(8,128)} async-done(((f32[128,8192]{1,0:T(8,128)}), f32[128,8192]{1,0:T(8,128)}) %all-reduce.3.cloned.1.call-update) | async-done | bytes 4194320
  1118.5 2.1 subtract_multiply_fusion
  1120.7 0.4 fusion.19
  1121.0 15.9 %psum.7 = bf16[64,128]{1,0:T(8,128)(2,1)S(1)} all-reduce(bf16[64,128]{1,0:T(8,128)(2,1)S(1)} %fusion.19), channel_id=1, replica_groups=mesh['rep'=4,'fsdp'=128] {'rep'}, use_global_device_ids=true, to_apply=%region_1.2 | all-reduce | flops 8192 | bytes 32768 | tf_op jit(solution)/shard_map/psum | solution.py:63
  1136.9 0.3 convolution_multiply_fusion
  1137.3 1.0 convert_bitcast_fusion
  1138.3 0.0 all-gather.7.cloned.1.call-update
  1138.3 197.8 %all-gather.5.cloned.1.call-done = bf16[128,1,8192]{2,1,0:T(2,128)(2,1)} async-done(((bf16[1,1,8192]{2,1,0:T(2,128)(2,1)}), bf16[128,1,8192]{2,1,0:T(2,128)(2,1)}) %all-gather.5.cloned.1.call-update) | async-done | bytes 2097168 | tf_op jit(solution)/shard_map/all_gather | solution.py:46
  1336.2 7.0 fusion.14
  1343.1 0.7 fusion.44
  1343.8 213.2 %all-gather.7.cloned.1.call-done = bf16[128,1,8192]{2,1,0:T(2,128)(2,1)} async-done(((bf16[1,1,8192]{2,1,0:T(2,128)(2,1)}), bf16[128,1,8192]{2,1,0:T(2,128)(2,1)}) %all-gather.7.cloned.1.call-update) | async-done | bytes 2097168 | tf_op jit(solution)/shard_map/all_gather | solution.py:70
  1557.0 5.4 fusion
  (16 shorter events, 0.0 us)
Async XLA Ops:
  7.2 0.8 copy-start
  7.2 1111.4 %all-reduce.3.cloned.1.call-start = ((), (), s32[]{:S(2)}) async-start(), calls=%async_computation.2 | async-start | bytes 8388608
  12.9 0.8 copy-start.3
  12.9 1105.6 %copy-start.1 = (f32[1,8192]{1,0:T(1,128)S(1)}, f32[1,8192]{1,0:T(1,128)}, u32[]{:S(2)}) copy-start(f32[1,8192]{1,0:T(1,128)} %param.13) | copy-start | bytes 98308
  12.9 1105.6 %copy-start.4 = (f32[1,1,8192]{2,1,0:T(1,128)S(1)}, f32[1,1,8192]{2,1,0:T(1,128)}, u32[]{:S(2)}) copy-start(f32[1,1,8192]{2,1,0:T(1,128)} %param.12) | copy-start | bytes 98308
  12.9 1105.6 %copy-start.5 = (f32[1,1,8192]{2,1,0:T(1,128)S(1)}, f32[1,1,8192]{2,1,0:T(1,128)}, u32[]{:S(2)}) copy-start(f32[1,1,8192]{2,1,0:T(1,128)} %param.11) | copy-start | bytes 98308
  12.9 1124.4 %copy-start.6 = (f32[1,8192]{1,0:T(1,128)S(1)}, f32[1,8192]{1,0:T(1,128)}, u32[]{:S(2)}) copy-start(f32[1,8192]{1,0:T(1,128)} %param.14) | copy-start | bytes 98308
  13.0 1323.2 %all-gather.5.cloned.1.call-start = ((), (), s32[]{:S(2)}) async-start(), calls=%async_computation | async-start | bytes 4227072 | tf_op jit(solution)/shard_map/all_gather | solution.py:46
  14.3 1542.7 %all-gather.7.cloned.1.call-start = ((), (), s32[]{:S(2)}) async-start(), calls=%async_computation.1 | async-start | bytes 4227072 | tf_op jit(solution)/shard_map/all_gather | solution.py:70
  1120.6 436.4 %copy-start.7 = (bf16[1,32,128]{2,1,0:T(8,128)(2,1)S(1)}, bf16[1,32,128]{2,1,0:T(8,128)(2,1)}, u32[]{:S(2)}) copy-start(bf16[1,32,128]{2,1,0:T(8,128)(2,1)} %param.15) | copy-start | bytes 24580
  1138.3 424.2 %copy-start.2 = (f32[1,8192]{1,0:T(1,128)}, f32[1,8192]{1,0:T(1,128)S(1)}, u32[]{:S(2)}) copy-start(f32[1,8192]{1,0:T(1,128)S(1)} %get-tuple-element.6) | copy-start | bytes 98308
Sparse Core Ops, SparseCore 0:
  13.1 1105.4 all-reduce.2
  1121.5 214.6 all-gather.4
  1339.1 217.8 all-gather.6
where the time goes:
time: 1570 us
  waiting for transfers between devices  1510 us (96%)
  matrix products  18 us (1%)
  blocking collectives  15.9 us (1%)
    unnamed x4, waiting for transfers between devices  1100 us
    all_gather x1, waiting for transfers between devices, shards(): all_merged = lax.all_gather(merged16, 'fsdp', axis=0, tiled=True)  213 us
    all_gather x1, waiting for transfers between devices, shards(): all_weights = lax.all_gather(weights16, 'fsdp', axis=0, tiled=True)  198 us
  transfers between devices with their start and end apart: 3, of which 3 were waited for; matrix products, arithmetic and copies ran while one was open for 1% of the time, Pallas kernels for 0%

commit v1 on v0

v1 whole, which is shorter than its diff:
```python
import functools
import math

import jax
import jax.numpy as jnp
from jax import lax
from jax.experimental import pallas as pl
from jax.experimental.pallas import tpu as pltpu
from jax.sharding import PartitionSpec as P

BETA_ONE = 0.9
BETA_TWO = 0.95
INNER_LR = 0.3
DECAY = 0.1
EPS = 1e-08
OUTER_LR = 0.7
MOMENTUM = 0.9
ALPHA = 0.5
STEP = 100

BF16 = jnp.bfloat16
F32 = jnp.float32


def row_table():
    p = lax.broadcasted_iota(jnp.int32, (128, 128), 0)
    f = lax.broadcasted_iota(jnp.int32, (128, 128), 1)
    x = lax.shift_right_logical(p, 5)
    y = lax.bitwise_and(lax.shift_right_logical(p, 2), 7)
    z = lax.bitwise_and(lax.shift_right_logical(p, 1), 1)
    c = lax.bitwise_and(p, 1)
    return jnp.where(f == z * 64 + y * 8 + x * 2 + c, 1.0, 0.0).astype(BF16)


def hadamard_table():
    i = lax.broadcasted_iota(jnp.int32, (128, 128), 0)
    j = lax.broadcasted_iota(jnp.int32, (128, 128), 1)
    bits = lax.bitwise_and(i, j)
    bits = lax.bitwise_xor(bits, lax.shift_right_logical(bits, 4))
    bits = lax.bitwise_xor(bits, lax.shift_right_logical(bits, 2))
    bits = lax.bitwise_xor(bits, lax.shift_right_logical(bits, 1))
    return (1 - 2 * lax.bitwise_and(bits, 1)).astype(F32)


def sign_table():
    j = lax.broadcasted_iota(jnp.int32, (64, 128), 0) * 128 + lax.broadcasted_iota(
        jnp.int32, (64, 128), 1
    )
    return (1 - 2 * lax.rem(lax.rem(97 * j, 251), 2)).astype(F32)


def rotate(values, table):
    out = jnp.dot(
        values, table, precision=lax.Precision.HIGHEST, preferred_element_type=F32
    )
    return out * (1.0 / math.sqrt(128.0))


def copy_to(src, dst, send_sem, recv_sem, device):
    return pltpu.make_async_remote_copy(
        src_ref=src,
        dst_ref=dst,
        send_sem=send_sem,
        recv_sem=recv_sem,
        device_id=device,
        device_id_type=pl.DeviceIdType.MESH,
    )


def aligned(index, size):
    return pl.ds(pl.multiple_of(index * size, size), size)


def kernel(
    hidden, cot, master, adam_m, adam_v, anchor, outer_mom, next_hidden,
    grad_hidden, merged_out, anchor_out, mom_out, next_out,
    cotv, part, core_send, core_recv, x_send, x_recv, rows, y_send, y_recv,
    zc_sum, zc_send, zc_recv, grad, rot, row16, ag_y, ag_rows, weights,
    cot_sem, core_ss, core_rs, x_ss, x_rs, y_ss, y_rs, zc_ss, zc_rs,
    rep_ss, rep_rs, agz_ss, agz_rs, agy_ss, agy_rs, agx_ss, agx_rs, agc_ss, agc_rs,
):
    rep = lax.axis_index("rep")
    me = lax.axis_index("fsdp")
    z = lax.div(me, 64)
    y = lax.rem(lax.div(me, 8), 8)
    x = lax.rem(lax.div(me, 2), 4)
    c = lax.rem(me, 2)

    def at(zz, yy, xx, cc):
        return {"fsdp": zz * 64 + yy * 8 + xx * 2 + cc}

    pairs = ((0, 1), (1, 0), (1, 1))

    def flip(index):
        dz, dc = pairs[index]
        return (1 - z if dz else z), (1 - c if dc else c)

    partner = at(z, y, x, 1 - c)
    x_peers = [lax.rem(x + d, 4) for d in range(1, 4)]
    x_from = [lax.rem(x + 4 - d, 4) for d in range(1, 4)]
    y_peers = [lax.rem(y + d, 8) for d in range(1, 8)]

    barrier = pltpu.get_barrier_semaphore()
    peers = [at(flip(i)[0], y, x, flip(i)[1]) for i in range(3)]
    peers += [at(z, y, xx, c) for xx in x_peers]
    peers += [at(z, yy, x, c) for yy in y_peers]
    peers += [{"rep": lax.rem(rep + d, 4)} for d in range(1, 4)]
    for peer in peers:
        pl.semaphore_signal(
            barrier, inc=1, device_id=peer, device_id_type=pl.DeviceIdType.MESH
        )

    halves = (1 - c, c)
    loads = []
    for h in range(2):
        for q in range(4):
            start = pl.multiple_of(halves[h] * 4096 + q * 1024, 1024)
            load = pltpu.make_async_copy(
                cot.at[:, pl.ds(start, 1024)], cotv.at[h, q], cot_sem.at[h * 4 + q]
            )
            load.start()
            loads.append(load)

    row16[0] = master[...].astype(BF16)
    order = row_table()
    turned = lax.dot_general(
        order, hidden[...], (((1,), (1,)), ((), ())), preferred_element_type=F32
    ).astype(BF16)

    pl.semaphore_wait(barrier, len(peers))
    sends = []

    def start(copy):
        copy.start()
        sends.append(copy)
        return copy

    def gather_zc(k):
        for i in range(3):
            zz, cc = flip(i)
            start(
                copy_to(
                    row16.at[k, aligned(cc, 32)],
                    ag_y.at[k, y, aligned(z * 2 + c, 32)],
                    agz_ss.at[k, i], agz_rs.at[k, i], at(zz, y, x, cc),
                )
            )
        ag_y[k, y, aligned(z * 2 + c, 32), :] = row16[k, aligned(c, 32), :]
        return sends[-3:]

    def gather_y(k, before):
        for copy in before:
            copy.wait_recv()
        for d in range(7):
            start(
                copy_to(
                    ag_y.at[k, y], ag_y.at[k, y],
                    agy_ss.at[k, d], agy_rs.at[k, d], at(z, y_peers[d], x, c),
                )
            )
        return sends[-7:]

    def gather_x(k, before):
        for copy in before:
            copy.wait_recv()
        ag_rows[k] = ag_y[k].reshape(1024, 128).astype(F32)
        mine = aligned(x, 32)
        for b in range(32):
            block = ag_rows[k, pl.ds(b, 32, stride=32), :]
            weights[k, 1, mine, b * 128 : (b + 1) * 128] = block.astype(BF16)
        copies = []
        for d in range(3):
            copies.append(
                start(
                    copy_to(
                        weights.at[k, 1, mine], weights.at[k, 1, mine],
                        agx_ss.at[k, d], agx_rs.at[k, d], at(z, y, x_peers[d], c),
                    )
                )
            )
        cores = [
            start(
                copy_to(
                    weights.at[k, 1, mine], weights.at[k, 0, mine],
                    agc_ss.at[k, 0], agc_rs.at[k, 0], partner,
                )
            )
        ]
        return copies, cores

    def gather_core(k, copies, cores):
        for d in range(3):
            copies[d].wait_recv()
            block = aligned(x_from[d], 32)
            cores.append(
                start(
                    copy_to(
                        weights.at[k, 1, block], weights.at[k, 0, block],
                        agc_ss.at[k, d + 1], agc_rs.at[k, d + 1], partner,
                    )
                )
            )
        return cores

    zc_copies = gather_zc(0)

    core_copies = []
    for q in range(4):
        loads[q].wait()
        core_send[q] = jnp.dot(
            turned, cotv[0, q], preferred_element_type=F32
        ).astype(BF16)
        core_copies.append(
            start(
                copy_to(
                    core_send.at[q], core_recv.at[q], core_ss.at[q], core_rs.at[q], partner
                )
            )
        )
    y_copies = gather_y(0, zc_copies)
    for q in range(4):
        loads[4 + q].wait()
        part[q] = jnp.dot(turned, cotv[1, q], preferred_element_type=F32)

    x_copies = []
    for q in range(4):
        core_copies[q].wait_recv()
        both = part[q] + core_recv[q].astype(F32)
        part[q] = both
        x_send[q] = both.astype(BF16)
        for d in range(3):
            x_copies.append(
                start(
                    copy_to(
                        x_send.at[q, aligned(x_peers[d], 32)], x_recv.at[q, d],
                        x_ss.at[q, d], x_rs.at[q, d], at(z, y, x_peers[d], c),
                    )
                )
            )
    for q in range(4):
        for d in range(3):
            x_copies[3 * q + d].wait_recv()
        total = part[q, aligned(x, 32), :]
        for d in range(3):
            total = total + x_recv[q, d].astype(F32)
        for b in range(8):
            rows[pl.ds(q * 8 + b, 32, stride=32), :] = total[:, b * 128 : (b + 1) * 128]

    y_send[...] = rows[...].astype(BF16)
    rs_y = []
    for d in range(7):
        rs_y.append(
            start(
                copy_to(
                    y_send.at[aligned(y_peers[d], 128)], y_recv.at[d],
                    y_ss.at[d], y_rs.at[d], at(z, y_peers[d], x, c),
                )
            )
        )
    x_gathers, c_gathers = gather_x(0, y_copies)

    total = rows[aligned(y, 128), :]
    for d in range(7):
        rs_y[d].wait_recv()
        total = total + y_recv[d].astype(F32)
    zc_sum[...] = total
    zc_send[...] = total.astype(BF16)
    rs_zc = []
    for i in range(3):
        zz, cc = flip(i)
        rs_zc.append(
            start(
                copy_to(
                    zc_send.at[aligned(zz * 2 + cc, 32)], zc_recv.at[i],
                    zc_ss.at[i], zc_rs.at[i], at(zz, y, x, cc),
                )
            )
        )
    table = hadamard_table()
    signs = sign_table()
    for copy in rs_zc:
        copy.wait_recv()
    grad[aligned(c, 32), :] = zc_sum[aligned(z * 2 + c, 32), :] + zc_recv[1].astype(F32)
    grad[aligned(1 - c, 32), :] = zc_recv[0].astype(F32) + zc_recv[2].astype(F32)

    gradient = grad[...]
    first = BETA_ONE * adam_m[...] + (1.0 - BETA_ONE) * gradient
    second = BETA_TWO * adam_v[...] + (1.0 - BETA_TWO) * gradient * gradient
    corr_one = 1.0 - BETA_ONE**STEP
    corr_two = 1.0 - BETA_TWO**STEP
    update = first / corr_one / (jnp.sqrt(second / corr_two) + EPS) + DECAY * master[...]
    inner = master[...] - INNER_LR * update
    rot[rep] = rotate((anchor[...] - inner) * signs, table).astype(BF16)
    rep_copies = []
    for d in range(3):
        rep_copies.append(
            start(
                copy_to(
                    rot.at[rep], rot.at[rep], rep_ss.at[d], rep_rs.at[d],
                    {"rep": lax.rem(rep + d + 1, 4)},
                )
            )
        )
    c_gathers = gather_core(0, x_gathers, c_gathers)
    for copy in rep_copies:
        copy.wait_recv()
    total = rot[0].astype(F32)
    for r in range(1, 4):
        total = total + rot[r].astype(F32)
    mean_delta = rotate(total, table) * signs * 0.25
    new_momentum = MOMENTUM * outer_mom[...] + mean_delta
    new_anchor = anchor[...] - OUTER_LR * (MOMENTUM * new_momentum + mean_delta)
    merged = ALPHA * inner + (1.0 - ALPHA) * new_anchor
    row16[1] = merged.astype(BF16)
    zc_copies = gather_zc(1)
    mom_out[...] = new_momentum
    anchor_out[...] = new_anchor
    merged_out[...] = merged
    y_copies = gather_y(1, zc_copies)

    for copy in c_gathers:
        copy.wait_recv()
    products = jnp.zeros((256, 128), F32)
    for h in range(2):
        for q in range(4):
            products = products + lax.dot_general(
                cotv[h, q], weights[0, h, :, q * 1024 : (q + 1) * 1024],
                (((1,), (1,)), ((), ())), preferred_element_type=F32,
            )
    grad_hidden[...] = jnp.dot(
        products.astype(BF16), order, preferred_element_type=F32
    ).astype(BF16)
    ahead = lax.dot_general(
        next_hidden[...], order, (((1,), (1,)), ((), ())), preferred_element_type=F32
    ).astype(BF16)

    x_gathers, c_gathers = gather_x(1, y_copies)
    c_gathers = gather_core(1, x_gathers, c_gathers)
    for q in range(4):
        start_col = pl.multiple_of(c * 4096 + q * 1024, 1024)
        next_out[:, pl.ds(start_col, 1024)] = jnp.dot(
            ahead, weights[1, 1, :, q * 1024 : (q + 1) * 1024], preferred_element_type=F32
        ).astype(BF16)
    for copy in c_gathers:
        copy.wait_recv()
    for q in range(4):
        start_col = pl.multiple_of((1 - c) * 4096 + q * 1024, 1024)
        next_out[:, pl.ds(start_col, 1024)] = jnp.dot(
            ahead, weights[1, 0, :, q * 1024 : (q + 1) * 1024], preferred_element_type=F32
        ).astype(BF16)
    for copy in sends:
        copy.wait_send()


def shards(hidden, cotangent, master, adam_m, adam_v, anchor, outer_mom, next_hidden):
    vmem = pl.BlockSpec(memory_space=pltpu.VMEM)
    dma = pltpu.SemaphoreType.DMA
    row = lambda a: a.reshape(64, 128)
    outs = pl.pallas_call(
        kernel,
        out_shape=(
            jax.ShapeDtypeStruct((256, 128), BF16),
            jax.ShapeDtypeStruct((64, 128), F32),
            jax.ShapeDtypeStruct((64, 128), F32),
            jax.ShapeDtypeStruct((64, 128), F32),
            jax.ShapeDtypeStruct((32, 8192), BF16),
        ),
        in_specs=[vmem, pl.BlockSpec(memory_space=pl.ANY)] + [vmem] * 6,
        out_specs=(vmem,) * 5,
        scratch_shapes=[
            pltpu.VMEM((2, 4, 256, 1024), BF16),
            pltpu.VMEM((4, 128, 1024), F32),
            pltpu.VMEM((4, 128, 1024), BF16),
            pltpu.VMEM((4, 128, 1024), BF16),
            pltpu.VMEM((4, 128, 1024), BF16),
            pltpu.VMEM((4, 3, 32, 1024), BF16),
            pltpu.VMEM((1024, 128), F32),
            pltpu.VMEM((1024, 128), BF16),
            pltpu.VMEM((7, 128, 128), BF16),
            pltpu.VMEM((128, 128), F32),
            pltpu.VMEM((128, 128), BF16),
            pltpu.VMEM((3, 32, 128), BF16),
            pltpu.VMEM((64, 128), F32),
            pltpu.VMEM((4, 64, 128), BF16),
            pltpu.VMEM((2, 64, 128), BF16),
            pltpu.VMEM((2, 8, 128, 128), BF16),
            pltpu.VMEM((2, 1024, 128), F32),
            pltpu.VMEM((2, 2, 128, 4096), BF16),
            dma((8,)),
            dma((4,)), dma((4,)), dma((4, 3)), dma((4, 3)), dma((7,)), dma((7,)),
            dma((3,)), dma((3,)), dma((3,)), dma((3,)), dma((2, 3)), dma((2, 3)),
            dma((2, 7)), dma((2, 7)), dma((2, 3)), dma((2, 3)), dma((2, 4)), dma((2, 4)),
        ],
        compiler_params=pltpu.CompilerParams(
            collective_id=0, has_side_effects=True, vmem_limit_bytes=48 * 1024 * 1024
        ),
        name="sync",
    )(
        hidden[0], cotangent[0], row(master), row(adam_m), row(adam_v),
        row(anchor), row(outer_mom), next_hidden[0],
    )
    grad_hidden, merged, new_anchor, new_momentum, next_out = outs
    return (
        grad_hidden[None],
        merged.reshape(1, 1, 8192),
        new_anchor.reshape(1, 8192),
        new_momentum.reshape(1, 8192),
        next_out[None],
    )


def solution(mesh):
    in_specs = (
        P("rep", "fsdp", None),
        P("rep", "fsdp", None),
        P("rep", "fsdp", None),
        P("rep", "fsdp", None),
        P("rep", "fsdp", None),
        P("fsdp", None),
        P("fsdp", None),
        P("rep", "fsdp", None),
    )
    out_specs = (
        P("rep", "fsdp", None),
        P("rep", "fsdp", None),
        P("fsdp", None),
        P("fsdp", None),
        P("rep", "fsdp", None),
    )
    return jax.shard_map(shards, mesh=mesh, in_specs=in_specs, out_specs=out_specs, check_vma=False)
```

time: 1570 us -> 91.5 us (0.06)
  waiting for transfers between devices: 1510 us -> 0 us
  Pallas kernels: 0 us -> 79.5 us
  matrix products: 18 us -> 0 us
  blocking collectives: 15.9 us -> 0 us
    unnamed x4 -> x0, waiting for transfers between devices: 1100 us -> none
    all_gather x2 -> x0, waiting for transfers between devices: 411 us -> none  [the longest x1 213 us: shards(): all_merged = lax.all_gather(merged16, 'fsdp', axis=0, tiled=True)]
    pallas_call x0 -> x1, Pallas kernels: none -> 79.5 us  [shards(): pl.pallas_call(kernel, out_shape=(jax.ShapeDtypeStruct((256, 128), BF16),...]
    dot_general x5 -> x0, matrix products: 18 us -> none  [the longest x1 6.96 us: shards(): lax.dot_general(cotangent_rows, all_weights, (((1,), (1,)), ((), ())), pr...]
    psum x1 -> x0, blocking collectives: 15.9 us -> none  [shards(): lax.psum(rotated.astype(jnp.float32).astype(jnp.bfloat16), 'rep')]
  transfers between devices with their start and end apart: 3 -> 0, of which waited for: 3 -> 0; matrix products, arithmetic and copies ran while one was open for 1% -> 0% of each run, Pallas kernels for 0% -> 0%
where the time goes in v1:
time: 91.5 us; the launch traced here: 90.9 us
  Pallas kernels  79.5 us (87%)
  local copies, waits for them, and re-layouts  10.8 us (12%)
    pallas_call x1, Pallas kernels, shards(): pl.pallas_call(kernel, out_shape=(jax.ShapeDtypeStruct((256, 128), BF16),...  79.5 us
    unnamed x21, local copies, waits for them, and re-layouts  10.8 us

profile of v1, /device:TPU:1, one launch (start us, length us, event | category | flops | bytes accessed | tf_op | source)
XLA Modules:
  0.0 90.9 jit_solution(12382263186574435208)
XLA Ops:
  0.6 0.0 copy-start
  0.6 2.2 %copy-done = bf16[1,256,8192]{2,1,0:T(8,128)(2,1)S(1)} copy-done((bf16[1,256,8192]{2,1,0:T(8,128)(2,1)S(1)}, bf16[1,256,8192]{2,1,0:T(8,128)(2,1)}, u32[]{:S(2)}) %copy-start) | copy-done | bytes 4194328
  2.8 0.0 copy-start.1
  2.8 0.8 copy-done.1
  3.7 0.0 copy-start.2
  3.7 0.8 copy-done.2
  4.4 0.0 copy-start.3
  4.4 0.8 copy-done.3
  5.2 0.0 copy-start.4
  5.2 0.8 copy-done.4
  5.9 0.0 copy-start.5
  5.9 0.8 copy-done.5
  6.7 0.0 copy-start.6
  6.7 0.8 copy-done.6
  7.5 0.0 copy-start.7
  7.5 0.7 copy-done.7
  8.2 79.5 %sync.1 = (bf16[256,128]{1,0:T(8,128)(2,1)S(1)}, f32[64,128]{1,0:T(8,128)S(1)}, f32[64,128]{1,0:T(8,128)S(1)}, f32[64,128]{1,0:T(8,128)S(1)}, bf16[32,8192]{1,0:T(8,128)(2,1)S(1)}) custom-call(bf16[256,128]{1,0:T(8,128)(2,1)S(1)} %bitcast.15, bf16[256,8192]{1,0:T(8,128)(2,1)S(1)} %bitcast.13, f32[64,128]{1,0:T(8,128)S(1)} %bitcast.17, ...), custom_call_target="tpu_custom_call" | custom-call | tf_op jit(solution)/shard_map/sync/pallas_call | solution.py:359
  87.6 0.6 copy.18
  88.3 0.6 copy.19
  88.9 0.6 copy.20
  89.5 0.6 copy.21
  90.1 0.8 copy.22
Async XLA Ops:
  0.6 2.2 %copy-start = (bf16[1,256,8192]{2,1,0:T(8,128)(2,1)S(1)}, bf16[1,256,8192]{2,1,0:T(8,128)(2,1)}, u32[]{:S(2)}) copy-start(bf16[1,256,8192]{2,1,0:T(8,128)(2,1)} %param.9) | copy-start | bytes 12582916
  2.8 0.8 copy-start.1
  3.7 0.8 copy-start.2
  4.4 0.8 copy-start.3
  5.2 0.8 copy-start.4
  5.9 0.8 copy-start.5
  6.7 0.8 copy-start.6
  7.5 0.7 copy-start.7

commit v2 on v1

v2 whole, which is shorter than its diff:
```python
import math

import jax
import jax.numpy as jnp
from jax import lax
from jax.experimental import pallas as pl
from jax.experimental.pallas import tpu as pltpu
from jax.sharding import PartitionSpec as P

BETA_ONE = 0.9
BETA_TWO = 0.95
INNER_LR = 0.3
DECAY = 0.1
EPS = 1e-08
OUTER_LR = 0.7
MOMENTUM = 0.9
ALPHA = 0.5
STEP = 100

BF16 = jnp.bfloat16
F32 = jnp.float32
VMEM_BYTES = 62 * 1024 * 1024
CHUNKS = 4
PARTS = 2
WIDE = 1024 // PARTS


def row_table():
    p = lax.broadcasted_iota(jnp.int32, (128, 128), 0)
    f = lax.broadcasted_iota(jnp.int32, (128, 128), 1)
    y = lax.shift_right_logical(p, 4)
    z = lax.bitwise_and(lax.shift_right_logical(p, 3), 1)
    return jnp.where(f == z * 64 + y * 8 + lax.bitwise_and(p, 7), 1.0, 0.0).astype(BF16)


def hadamard_table():
    i = lax.broadcasted_iota(jnp.int32, (128, 128), 0)
    j = lax.broadcasted_iota(jnp.int32, (128, 128), 1)
    bits = lax.bitwise_and(i, j)
    bits = lax.bitwise_xor(bits, lax.shift_right_logical(bits, 4))
    bits = lax.bitwise_xor(bits, lax.shift_right_logical(bits, 2))
    bits = lax.bitwise_xor(bits, lax.shift_right_logical(bits, 1))
    return (1 - 2 * lax.bitwise_and(bits, 1)).astype(F32)


def sign_table():
    j = lax.broadcasted_iota(jnp.int32, (64, 128), 0) * 128 + lax.broadcasted_iota(
        jnp.int32, (64, 128), 1
    )
    return (1 - 2 * lax.rem(lax.rem(97 * j, 251), 2)).astype(F32)


def rotate(values, table):
    out = jnp.dot(
        values, table, precision=lax.Precision.HIGHEST, preferred_element_type=F32
    )
    return out * (1.0 / math.sqrt(128.0))


def copy_to(src, dst, send_sem, recv_sem, device):
    return pltpu.make_async_remote_copy(
        src_ref=src,
        dst_ref=dst,
        send_sem=send_sem,
        recv_sem=recv_sem,
        device_id=device,
        device_id_type=pl.DeviceIdType.MESH,
    )


def aligned(index, size):
    return pl.ds(pl.multiple_of(index * size, size), size)


def kernel(
    hidden_in, cot, master_in, adam_m_in, adam_v_in, anchor_in, outer_mom_in, next_in,
    grad_hidden_out, merged_out, anchor_out, mom_out, next_out,
    grad_hidden, results, hidden, state, next_all, cotv, core_send, core_recv,
    part, x_send, x_recv, x_sum, y_send, y_recv, line_send, line_recv, grad, rot,
    row, ag_in, gathered, weights, ahead_send, ahead_out,
    out_sem, next_sem, in_sem, state_sem, cot_sem, nh_ss, nh_rs, core_ss, core_rs,
    x_ss, x_rs, y_ss, y_rs, line_ss, line_rs, rep_ss, rep_rs, ag_ss, ag_rs,
    agy_ss, agy_rs, agx_ss, agx_rs, agc_ss, agc_rs, last_ss, last_rs,
):
    rep = lax.axis_index("rep")
    me = lax.axis_index("fsdp")
    z = lax.div(me, 64)
    y = lax.rem(lax.div(me, 8), 8)
    x = lax.rem(lax.div(me, 2), 4)
    c = lax.rem(me, 2)

    def at(zz, yy, xx, cc):
        return {"fsdp": zz * 64 + yy * 8 + xx * 2 + cc}

    group = []
    for dz in range(2):
        for dx in range(4):
            for dc in range(2):
                if dz or dx or dc:
                    group.append(
                        (1 - z if dz else z, lax.rem(x + dx, 4), 1 - c if dc else c)
                    )
    plane = group[:7]
    partner = at(z, y, x, 1 - c)
    x_peers = [lax.rem(x + d, 4) for d in range(1, 4)]
    x_from = [lax.rem(x + 4 - d, 4) for d in range(1, 4)]
    y_peers = [lax.rem(y + d, 8) for d in range(1, 8)]

    barrier = pltpu.get_barrier_semaphore()
    peers = [at(zz, y, xx, cc) for zz, xx, cc in group]
    peers += [at(z, yy, x, c) for yy in y_peers]
    peers += [{"rep": lax.rem(rep + d, 4)} for d in range(1, 4)]
    for peer in peers:
        pl.semaphore_signal(
            barrier, inc=1, device_id=peer, device_id_type=pl.DeviceIdType.MESH
        )

    sends = []

    def start(copy):
        copy.start()
        sends.append(copy)
        return copy

    halves = (1 - c, c)
    seat = aligned(x * 2 + c, 32)
    loads = [
        pltpu.make_async_copy(hidden_in, hidden, in_sem.at[0]),
        pltpu.make_async_copy(master_in, state.at[0], in_sem.at[1]),
        pltpu.make_async_copy(next_in, next_all.at[seat], in_sem.at[2]),
    ]
    for load in loads:
        load.start()
    cot_loads = {}
    for h in range(2):
        for j in range(CHUNKS):
            for s in range(4):
                begin = pl.multiple_of(halves[h] * 4096 + s * 1024 + j * 256, 256)
                load = pltpu.make_async_copy(
                    cot.at[:, pl.ds(begin, 256)],
                    cotv.at[h, j, :, pl.ds(s * 256, 256)],
                    cot_sem.at[h, j, s],
                )
                load.start()
                cot_loads[h, j, s] = load
    late_loads = [
        pltpu.make_async_copy(source, state.at[i + 1], state_sem.at[i])
        for i, source in enumerate((adam_m_in, adam_v_in, anchor_in, outer_mom_in))
    ]
    for load in late_loads:
        load.start()
    master, adam_m, adam_v, anchor, outer_mom = (state.at[i] for i in range(5))

    order = row_table()
    loads[0].wait()
    turned = lax.dot_general(
        order, hidden[...], (((1,), (1,)), ((), ())), preferred_element_type=F32
    ).astype(BF16)

    def gather_lines(k):
        copies = []
        for i, (zz, xx, cc) in enumerate(group):
            copies.append(
                start(
                    copy_to(
                        row.at[k, aligned(cc * 4 + xx, 8)],
                        ag_in.at[k, aligned(z * 8 + x * 2 + c, 8)],
                        ag_ss.at[k, i], ag_rs.at[k, i], at(zz, y, xx, cc),
                    )
                )
            )
        ag_in[k, aligned(z * 8 + x * 2 + c, 8), :] = row[k, aligned(c * 4 + x, 8), :]
        return copies

    def gather_y(k, before, parts):
        for copy in before:
            copy.wait_recv()
        mine = aligned(y, 16)
        for b in range(8):
            block = ag_in[k, pl.ds(b, 16, stride=8), :]
            gathered[k, mine, b * 128 : (b + 1) * 128] = block.astype(BF16)
        copies = []
        for q in range(parts):
            cols = pl.ds(q * (1024 // parts), 1024 // parts)
            for d in range(7):
                copies.append(
                    start(
                        copy_to(
                            gathered.at[k, mine, cols], gathered.at[k, mine, cols],
                            agy_ss.at[k, q, d], agy_rs.at[k, q, d], at(z, y_peers[d], x, c),
                        )
                    )
                )
        return copies

    core_copies = []
    for j in range(CHUNKS):
        for s in range(4):
            cot_loads[0, j, s].wait()
        core_send[j] = jnp.dot(turned, cotv[0, j], preferred_element_type=F32).astype(BF16)
        if j == 0:
            pl.semaphore_wait(barrier, len(peers))
        core_copies.append(
            start(
                copy_to(
                    core_send.at[j], core_recv.at[j], core_ss.at[j], core_rs.at[j], partner
                )
            )
        )
    x_copies = []
    for j in range(CHUNKS):
        for s in range(4):
            cot_loads[1, j, s].wait()
        own = jnp.dot(turned, cotv[1, j], preferred_element_type=F32)
        core_copies[j].wait_recv()
        both = own + core_recv[j].astype(F32)
        part[j] = both
        x_send[j] = both.astype(BF16)
        for d in range(3):
            x_copies.append(
                start(
                    copy_to(
                        x_send.at[j, :, aligned(x_peers[d], 256)], x_recv.at[j, d],
                        x_ss.at[j, d], x_rs.at[j, d], at(z, y, x_peers[d], c),
                    )
                )
            )

    loads[1].wait()
    row[0] = master[...].astype(BF16).astype(F32)
    line_copies = gather_lines(0)
    loads[2].wait()
    nh_copies = []
    for i, (zz, xx, cc) in enumerate(plane):
        nh_copies.append(
            start(
                copy_to(
                    next_all.at[seat], next_all.at[seat],
                    nh_ss.at[i], nh_rs.at[i], at(zz, y, xx, cc),
                )
            )
        )
    agy_copies = gather_y(0, line_copies, 1)

    rs_y = []
    for j in range(CHUNKS):
        total = part[j, :, aligned(x, 256)]
        for d in range(3):
            x_copies[3 * j + d].wait_recv()
            total = total + x_recv[j, d].astype(F32)
        x_sum[j] = total
        y_send[j] = total.astype(BF16)
        for d in range(7):
            rs_y.append(
                start(
                    copy_to(
                        y_send.at[j, aligned(y_peers[d], 16)], y_recv.at[j, d],
                        y_ss.at[j, d], y_rs.at[j, d], at(z, y_peers[d], x, c),
                    )
                )
            )

    for copy in agy_copies:
        copy.wait_recv()
    agx_copies, agc_copies = [], []
    for d in range(3):
        agx_copies.append(
            start(
                copy_to(
                    gathered.at[0], weights.at[1, x],
                    agx_ss.at[d], agx_rs.at[d], at(z, y, x_peers[d], c),
                )
            )
        )
    agc_copies.append(
        start(
            copy_to(gathered.at[0], weights.at[0, x], agc_ss.at[0], agc_rs.at[0], partner)
        )
    )
    weights[1, x] = gathered[0]

    for j in range(CHUNKS):
        total = x_sum[j, aligned(y, 16), :]
        for d in range(7):
            rs_y[7 * j + d].wait_recv()
            total = total + y_recv[j, d].astype(F32)
        for b in range(2):
            line_send[pl.ds(2 * j + b, 16, stride=8), :] = total[:, b * 128 : (b + 1) * 128]
    rs_lines = []
    mine = aligned(z * 8 + x * 2 + c, 8)
    for i, (zz, xx, cc) in enumerate(group):
        rs_lines.append(
            start(
                copy_to(
                    line_send.at[aligned(zz * 8 + xx * 2 + cc, 8)], line_recv.at[mine],
                    line_ss.at[i], line_rs.at[i], at(zz, y, xx, cc),
                )
            )
        )
    line_recv[mine, :] = line_send[mine, :]
    table = hadamard_table()
    signs = sign_table()
    for load in late_loads:
        load.wait()
    for copy in rs_lines:
        copy.wait_recv()
    for cc in range(2):
        for xx in range(4):
            low, high = (xx * 2 + cc) * 8, (8 + xx * 2 + cc) * 8
            grad[(cc * 4 + xx) * 8 : (cc * 4 + xx + 1) * 8, :] = (
                line_recv[low : low + 8, :] + line_recv[high : high + 8, :]
            )

    gradient = grad[...]
    first = BETA_ONE * adam_m[...] + (1.0 - BETA_ONE) * gradient
    second = BETA_TWO * adam_v[...] + (1.0 - BETA_TWO) * gradient * gradient
    corr_one = 1.0 - BETA_ONE**STEP
    corr_two = 1.0 - BETA_TWO**STEP
    update = first / corr_one / (jnp.sqrt(second / corr_two) + EPS) + DECAY * master[...]
    inner = master[...] - INNER_LR * update
    rot[rep] = rotate((anchor[...] - inner) * signs, table).astype(BF16)
    rep_copies = []
    for d in range(3):
        rep_copies.append(
            start(
                copy_to(
                    rot.at[rep], rot.at[rep], rep_ss.at[d], rep_rs.at[d],
                    {"rep": lax.rem(rep + d + 1, 4)},
                )
            )
        )
    for copy in nh_copies:
        copy.wait_recv()
    ahead = lax.dot_general(
        next_all[...], order, (((1,), (1,)), ((), ())), preferred_element_type=F32
    ).astype(BF16)
    for copy in rep_copies:
        copy.wait_recv()
    total = rot[0].astype(F32)
    for r in range(1, 4):
        total = total + rot[r].astype(F32)
    mean_delta = rotate(total, table) * signs * 0.25
    new_momentum = MOMENTUM * outer_mom[...] + mean_delta
    new_anchor = anchor[...] - OUTER_LR * (MOMENTUM * new_momentum + mean_delta)
    merged = ALPHA * inner + (1.0 - ALPHA) * new_anchor
    row[1] = merged.astype(BF16).astype(F32)
    line_copies = gather_lines(1)
    results[0] = merged
    results[1] = new_anchor
    results[2] = new_momentum
    stores = [
        pltpu.make_async_copy(results.at[i], out, out_sem.at[i])
        for i, out in enumerate((merged_out, anchor_out, mom_out))
    ]
    for store in stores:
        store.start()
    agy_copies = gather_y(1, line_copies, PARTS)

    for d in range(3):
        agx_copies[d].wait_recv()
        agc_copies.append(
            start(
                copy_to(
                    weights.at[1, x_from[d]], weights.at[0, x_from[d]],
                    agc_ss.at[d + 1], agc_rs.at[d + 1], partner,
                )
            )
        )

    def times_weights(h):
        products = jnp.zeros((256, 128), F32)
        for j in range(CHUNKS):
            for s in range(4):
                products = products + lax.dot_general(
                    cotv[h, j, :, s * 256 : (s + 1) * 256],
                    weights[h, s, :, j * 256 : (j + 1) * 256],
                    (((1,), (1,)), ((), ())), preferred_element_type=F32,
                )
        return products

    products = times_weights(1)

    here = c * 4 + x
    last = []
    for q in range(PARTS):
        for d in range(7):
            agy_copies[7 * q + d].wait_recv()
        ahead_send[q] = jnp.dot(
            ahead, gathered[1, :, q * WIDE : (q + 1) * WIDE], preferred_element_type=F32
        ).astype(BF16)
        for i, (zz, xx, cc) in enumerate(plane):
            last.append(
                start(
                    copy_to(
                        ahead_send.at[q, aligned(xx * 2 + cc, 32)], ahead_out.at[here, q],
                        last_ss.at[q, i], last_rs.at[q, i], at(zz, y, xx, cc),
                    )
                )
            )

    for copy in agc_copies:
        copy.wait_recv()
    products = products + times_weights(0)
    grad_hidden[...] = jnp.dot(
        products.astype(BF16), order, preferred_element_type=F32
    ).astype(BF16)
    store = pltpu.make_async_copy(grad_hidden, grad_hidden_out, out_sem.at[3])
    store.start()
    stores.append(store)

    sources = []
    for dx in range(4):
        for dc in range(2):
            if dx or dc:
                sources.append((lax.rem(x + 4 - dx, 4), 1 - c if dc else c))
    for q in range(PARTS):
        for i in range(-1, 7):
            if i < 0:
                piece = here
                view = ahead_send.at[q, seat]
            else:
                last[7 * q + i].wait_recv()
                piece = sources[i][1] * 4 + sources[i][0]
                view = ahead_out.at[piece, q]
            begin = pl.multiple_of(piece * 1024 + q * WIDE, WIDE)
            store = pltpu.make_async_copy(
                view, next_out.at[:, pl.ds(begin, WIDE)], next_sem.at[q, i + 1]
            )
            store.start()
            stores.append(store)
    for store in stores:
        store.wait()
    for copy in sends:
        copy.wait_send()


def store_kernel(*refs):
    sources, outs, held, sems = refs[:5], refs[5:10], refs[10:15], refs[15]
    inward = [pltpu.make_async_copy(a, b, sems.at[0, i]) for i, (a, b) in enumerate(zip(sources, held))]
    outward = [pltpu.make_async_copy(a, b, sems.at[1, i]) for i, (a, b) in enumerate(zip(held, outs))]
    for copy in inward:
        copy.start()
    for come, go in zip(inward, outward):
        come.wait()
        go.start()
    for copy in outward:
        copy.wait()


def shards(hidden, cotangent, master, adam_m, adam_v, anchor, outer_mom, next_hidden):
    hbm = pl.BlockSpec(memory_space=pltpu.HBM)
    dma = lambda *shape: pltpu.SemaphoreType.DMA(shape)
    row = lambda a: a.reshape(64, 128)
    shapes = (
        jax.ShapeDtypeStruct((256, 128), BF16),
        jax.ShapeDtypeStruct((64, 128), F32),
        jax.ShapeDtypeStruct((64, 128), F32),
        jax.ShapeDtypeStruct((64, 128), F32),
        jax.ShapeDtypeStruct((32, 8192), BF16),
    )
    outs = pl.pallas_call(
        kernel,
        out_shape=shapes,
        in_specs=[hbm] * 8,
        out_specs=(hbm,) * 5,
        scratch_shapes=[
            pltpu.VMEM((256, 128), BF16),
            pltpu.VMEM((3, 64, 128), F32),
            pltpu.VMEM((256, 128), BF16),
            pltpu.VMEM((5, 64, 128), F32),
            pltpu.VMEM((256, 128), BF16),
            pltpu.VMEM((2, CHUNKS, 256, 1024), BF16),
            pltpu.VMEM((CHUNKS, 128, 1024), BF16),
            pltpu.VMEM((CHUNKS, 128, 1024), BF16),
            pltpu.VMEM((CHUNKS, 128, 1024), F32),
            pltpu.VMEM((CHUNKS, 128, 1024), BF16),
            pltpu.VMEM((CHUNKS, 3, 128, 256), BF16),
            pltpu.VMEM((CHUNKS, 128, 256), F32),
            pltpu.VMEM((CHUNKS, 128, 256), BF16),
            pltpu.VMEM((CHUNKS, 7, 16, 256), BF16),
            pltpu.VMEM((128, 128), F32),
            pltpu.VMEM((128, 128), F32),
            pltpu.VMEM((64, 128), F32),
            pltpu.VMEM((4, 64, 128), BF16),
            pltpu.VMEM((2, 64, 128), F32),
            pltpu.VMEM((2, 128, 128), F32),
            pltpu.VMEM((2, 128, 1024), BF16),
            pltpu.VMEM((2, 4, 128, 1024), BF16),
            pltpu.VMEM((PARTS, 256, WIDE), BF16),
            pltpu.VMEM((8, PARTS, 32, WIDE), BF16),
            dma(4), dma(PARTS, 8), dma(3), dma(4), dma(2, CHUNKS, 4), dma(7), dma(7),
            dma(CHUNKS), dma(CHUNKS), dma(CHUNKS, 3), dma(CHUNKS, 3),
            dma(CHUNKS, 7), dma(CHUNKS, 7), dma(15), dma(15), dma(3), dma(3),
            dma(2, 15), dma(2, 15), dma(2, PARTS, 7), dma(2, PARTS, 7),
            dma(3), dma(3), dma(4), dma(4), dma(PARTS, 7), dma(PARTS, 7),
        ],
        compiler_params=pltpu.CompilerParams(
            collective_id=0, has_side_effects=True, vmem_limit_bytes=VMEM_BYTES
        ),
        name="sync",
    )(
        hidden[0], cotangent[0], row(master), row(adam_m), row(adam_v),
        row(anchor), row(outer_mom), next_hidden[0],
    )
    outs = pl.pallas_call(
        store_kernel,
        out_shape=shapes,
        in_specs=[hbm] * 5,
        out_specs=(hbm,) * 5,
        scratch_shapes=[pltpu.VMEM(s.shape, s.dtype) for s in shapes] + [dma(2, 5)],
        compiler_params=pltpu.CompilerParams(vmem_limit_bytes=VMEM_BYTES),
        name="store",
    )(*outs)
    grad_hidden, merged, new_anchor, new_momentum, next_out = outs
    return (
        grad_hidden[None],
        merged.reshape(1, 1, 8192),
        new_anchor.reshape(1, 8192),
        new_momentum.reshape(1, 8192),
        next_out[None],
    )


def solution(mesh):
    in_specs = (
        P("rep", "fsdp", None),
        P("rep", "fsdp", None),
        P("rep", "fsdp", None),
        P("rep", "fsdp", None),
        P("rep", "fsdp", None),
        P("fsdp", None),
        P("fsdp", None),
        P("rep", "fsdp", None),
    )
    out_specs = (
        P("rep", "fsdp", None),
        P("rep", "fsdp", None),
        P("fsdp", None),
        P("fsdp", None),
        P("rep", "fsdp", None),
    )
    return jax.shard_map(shards, mesh=mesh, in_specs=in_specs, out_specs=out_specs, check_vma=False)
```

time: 91.5 us -> 86 us (0.940)
  local copies, waits for them, and re-layouts: 10.8 us -> 0 us
  Pallas kernels: 79.5 us -> 85.2 us
    unnamed x21 -> x0, local copies, waits for them, and re-layouts: 10.8 us -> none
    pallas_call x1 -> x2, Pallas kernels: 79.5 us -> 85.2 us  [the longest x1 83.1 us: shards(): pl.pallas_call(kernel, out_shape=shapes, in_specs=[hbm] * 8, out_specs=(h...]
where the time goes in v2:
time: 86 us; the launch traced here: 85.8 us
  Pallas kernels  85.2 us (99%)
    pallas_call x1, Pallas kernels, shards(): pl.pallas_call(kernel, out_shape=shapes, in_specs=[hbm] * 8, out_specs=(h...  83.1 us
    pallas_call x1, Pallas kernels, shards(): pl.pallas_call(store_kernel, out_shape=shapes, in_specs=[hbm] * 5, out_sp...  2.02 us

profile of v2, /device:TPU:1, one launch (start us, length us, event | category | flops | bytes accessed | tf_op | source)
XLA Modules:
  0.0 85.8 jit_solution(14370737044284756365)
XLA Ops:
  0.6 83.1 %sync.1 = (bf16[256,128]{1,0:T(8,128)(2,1)}, f32[64,128]{1,0:T(8,128)}, f32[64,128]{1,0:T(8,128)}, f32[64,128]{1,0:T(8,128)}, bf16[32,8192]{1,0:T(8,128)(2,1)}) custom-call(bf16[256,128]{1,0:T(8,128)(2,1)} %bitcast.14, bf16[256,8192]{1,0:T(8,128)(2,1)} %bitcast.13, f32[64,128]{1,0:T(8,128)} %bitcast.15, f32[64,128]{1,0:T(8,128)} %bitcast.16, ...), custom_call_target="tpu_custom_call" | custom-call | tf_op jit(solution)/shard_map/sync/pallas_call | solution.py:461
  83.8 2.0 %store.1 = (bf16[256,128]{1,0:T(8,128)(2,1)}, f32[64,128]{1,0:T(8,128)}, f32[64,128]{1,0:T(8,128)}, f32[64,128]{1,0:T(8,128)}, bf16[32,8192]{1,0:T(8,128)(2,1)}) custom-call(bf16[256,128]{1,0:T(8,128)(2,1)} %get-tuple-element.15.refs_0_, f32[64,128]{1,0:T(8,128)} %get-tuple-element.16.refs_1_, f32[64,128]{1,0:T(8,128)} %get-tuple-element.17.refs_2_, ...), custom_call_target="tpu_custom_call" | custom-call | tf_op jit(solution)/shard_map/store/pallas_call | solution.py:505

commit v3 on v2

v3 whole, which is shorter than its diff:
```python
import math

import jax
import jax.numpy as jnp
from jax import lax
from jax.experimental import pallas as pl
from jax.experimental.pallas import tpu as pltpu
from jax.sharding import PartitionSpec as P

BETA_ONE = 0.9
BETA_TWO = 0.95
INNER_LR = 0.3
DECAY = 0.1
EPS = 1e-08
OUTER_LR = 0.7
MOMENTUM = 0.9
ALPHA = 0.5
STEP = 100

BF16 = jnp.bfloat16
F32 = jnp.float32
VMEM_BYTES = 62 * 1024 * 1024
CHUNKS = 4
PARTS = 2
WIDE = 512 // PARTS
ARRAYS = 24


def row_table():
    p = lax.broadcasted_iota(jnp.int32, (128, 128), 0)
    f = lax.broadcasted_iota(jnp.int32, (128, 128), 1)
    y = lax.shift_right_logical(p, 4)
    z = lax.bitwise_and(lax.shift_right_logical(p, 3), 1)
    return jnp.where(f == z * 64 + y * 8 + lax.bitwise_and(p, 7), 1.0, 0.0).astype(BF16)


def hadamard_table():
    i = lax.broadcasted_iota(jnp.int32, (128, 128), 0)
    j = lax.broadcasted_iota(jnp.int32, (128, 128), 1)
    bits = lax.bitwise_and(i, j)
    bits = lax.bitwise_xor(bits, lax.shift_right_logical(bits, 4))
    bits = lax.bitwise_xor(bits, lax.shift_right_logical(bits, 2))
    bits = lax.bitwise_xor(bits, lax.shift_right_logical(bits, 1))
    return (1 - 2 * lax.bitwise_and(bits, 1)).astype(F32)


def sign_table(first):
    i = lax.broadcasted_iota(jnp.int32, (64, 128), 0)
    j = lax.broadcasted_iota(jnp.int32, (64, 128), 1)
    j = j + 128 * lax.shift_right_logical(i, 4) + first
    return (1 - 2 * lax.rem(lax.rem(97 * j, 251), 2)).astype(F32)


def rotate(values, table):
    out = jnp.dot(
        values, table, precision=lax.Precision.HIGHEST, preferred_element_type=F32
    )
    return out * (1.0 / math.sqrt(128.0))


def copy_to(src, dst, send_sem, recv_sem, device):
    return pltpu.make_async_remote_copy(
        src_ref=src,
        dst_ref=dst,
        send_sem=send_sem,
        recv_sem=recv_sem,
        device_id=device,
        device_id_type=pl.DeviceIdType.MESH,
    )


def aligned(index, size):
    return pl.ds(pl.multiple_of(index * size, size), size)


def kernel(
    hidden_in, cot, master_in, adam_m_in, adam_v_in, anchor_in, outer_mom_in, next_in,
    grad_hidden_out, merged_out, anchor_out, mom_out, next_out,
    grad_hidden, results, hidden, state, next_all, cotv, core_send, core_recv,
    part, x_send, x_recv, x_sum, y_send, y_recv, packed, state_in, rot,
    row16, half_in, half_rows, gathered, back_send, back_recv, weights, ahead_send, ahead_out,
    out_sem, next_sem, in_sem, state_sem, cot_sem, nh_ss, nh_rs, core_ss, core_rs,
    x_ss, x_rs, y_ss, y_rs, st_ss, st_rs, rep_ss, rep_rs, back_ss, back_rs,
    agy_ss, agy_rs, half_ss, half_rs, ring_ss, ring_rs, agc_ss, agc_rs, last_ss, last_rs,
):
    rep = lax.axis_index("rep")
    me = lax.axis_index("fsdp")
    z = lax.div(me, 64)
    y = lax.rem(lax.div(me, 8), 8)
    x = lax.rem(lax.div(me, 2), 4)
    c = lax.rem(me, 2)

    def at(zz, yy, xx, cc):
        return {"fsdp": zz * 64 + yy * 8 + xx * 2 + cc}

    group = []
    for dz in range(2):
        for dx in range(4):
            for dc in range(2):
                if dz or dx or dc:
                    group.append(
                        (1 - z if dz else z, lax.rem(x + dx, 4), 1 - c if dc else c)
                    )
    place = z * 8 + x * 2 + c
    slice_here = c * 8 + x * 2 + z
    partner = at(z, y, x, 1 - c)
    x_peers = [lax.rem(x + d, 4) for d in range(1, 4)]
    x_from = [lax.rem(x + 4 - d, 4) for d in range(1, 4)]
    y_peers = [lax.rem(y + d, 8) for d in range(1, 8)]

    barrier = pltpu.get_barrier_semaphore()
    peers = [at(zz, y, xx, cc) for zz, xx, cc in group]
    peers += [at(z, yy, x, c) for yy in y_peers]
    peers += [at(1 - z, yy, x, c) for yy in y_peers]
    peers += [{"rep": lax.rem(rep + d, 4)} for d in range(1, 4)]
    for peer in peers:
        pl.semaphore_signal(
            barrier, inc=1, device_id=peer, device_id_type=pl.DeviceIdType.MESH
        )

    sends = []

    def start(copy):
        copy.start()
        sends.append(copy)
        return copy

    halves = (1 - c, c)
    seat = aligned(place, 32)
    loads = [
        pltpu.make_async_copy(hidden_in, hidden, in_sem.at[0]),
        pltpu.make_async_copy(master_in, state.at[0], in_sem.at[1]),
        pltpu.make_async_copy(next_in, next_all.at[seat], in_sem.at[2]),
    ]
    for load in loads:
        load.start()
    chunk_at = [(1 - z if j < 2 else z) * 512 + j % 2 * 256 for j in range(CHUNKS)]
    cot_loads = {}
    for h in range(2):
        for j in range(CHUNKS):
            for s in range(4):
                begin = pl.multiple_of(halves[h] * 4096 + s * 1024 + chunk_at[j], 256)
                load = pltpu.make_async_copy(
                    cot.at[:, pl.ds(begin, 256)],
                    cotv.at[h, j, :, pl.ds(s * 256, 256)],
                    cot_sem.at[h, j, s],
                )
                load.start()
                cot_loads[h, j, s] = load
    late_loads = [
        pltpu.make_async_copy(source, state.at[i + 1], state_sem.at[i])
        for i, source in enumerate((adam_m_in, adam_v_in, anchor_in, outer_mom_in))
    ]
    for load in late_loads:
        load.start()

    order = row_table()
    loads[0].wait()
    turned = lax.dot_general(
        order, hidden[...], (((1,), (1,)), ((), ())), preferred_element_type=F32
    ).astype(BF16)

    y_up, y_down = at(z, y_peers[0], x, c), at(z, y_peers[6], x, c)

    def block_of(distance):
        return aligned(lax.rem(y + 8 + distance, 8), 16)

    half_copies, agc_copies, ring = [], [], {}

    def weights_start():
        loads[1].wait()
        row16[...] = state[0].astype(BF16)
        for i, (zz, xx, cc) in enumerate(group):
            half_copies.append(
                start(
                    copy_to(
                        row16.at[aligned(cc, 32)], half_in.at[place],
                        half_ss.at[i], half_rs.at[i], at(zz, y, xx, cc),
                    )
                )
            )
        half_in[place] = row16[aligned(c, 32), :]

    def to_partner(distance):
        i = len(agc_copies)
        block = block_of(distance)
        agc_copies.append(
            start(
                copy_to(
                    weights.at[1, block], weights.at[0, block],
                    agc_ss.at[i], agc_rs.at[i], partner,
                )
            )
        )

    def weights_step(step):
        if step == 1:
            for copy in half_copies:
                copy.wait_recv()
            half_rows[...] = half_in[...].reshape(512, 128).astype(F32)
            for b in range(32):
                block = half_rows[pl.ds(b, 16, stride=32), :]
                weights[1, block_of(0), b * 128 : (b + 1) * 128] = block.astype(BF16)
        for way, device in ((1, y_up), (-1, y_down)):
            side = 0 if way == 1 else 1
            if step > 1:
                ring[step - 1, way].wait_recv()
            if step == 5:
                continue
            view = weights.at[1, block_of(-way * (step - 1))]
            if step == 4:
                view = view.at[:, pl.ds(side * 2048, 2048)]
            ring[step, way] = start(
                copy_to(view, view, ring_ss.at[side, step - 1], ring_rs.at[side, step - 1], device)
            )
        if step == 1:
            to_partner(0)
        elif step == 5:
            to_partner(4)
        else:
            to_partner(1 - step)
            to_partner(step - 1)

    core_copies = []
    for j in range(CHUNKS):
        for s in range(4):
            cot_loads[0, j, s].wait()
        core_send[j] = jnp.dot(turned, cotv[0, j], preferred_element_type=F32).astype(BF16)
        if j == 0:
            pl.semaphore_wait(barrier, len(peers))
        core_copies.append(
            start(
                copy_to(
                    core_send.at[j], core_recv.at[j], core_ss.at[j], core_rs.at[j], partner
                )
            )
        )
    weights_start()

    for load in late_loads:
        load.wait()
    for i in range(16):
        for a in range(5):
            packed[i * ARRAYS + 4 * a : i * ARRAYS + 4 * a + 4, :] = state[a, 4 * i : 4 * i + 4, :]
        packed[i * ARRAYS + 20 : i * ARRAYS + 24, :] = jnp.zeros((4, 128), F32)
    state_copies, nh_copies = [], []
    loads[2].wait()
    for i, (zz, xx, cc) in enumerate(group):
        state_copies.append(
            start(
                copy_to(
                    packed.at[aligned(cc * 8 + xx * 2 + zz, ARRAYS)],
                    state_in.at[aligned(place, ARRAYS)],
                    st_ss.at[i], st_rs.at[i], at(zz, y, xx, cc),
                )
            )
        )
        nh_copies.append(
            start(
                copy_to(
                    next_all.at[seat], next_all.at[seat],
                    nh_ss.at[i], nh_rs.at[i], at(zz, y, xx, cc),
                )
            )
        )
    state_in[aligned(place, ARRAYS), :] = packed[aligned(slice_here, ARRAYS), :]

    x_copies = []
    for j in range(CHUNKS):
        for s in range(4):
            cot_loads[1, j, s].wait()
        own = jnp.dot(turned, cotv[1, j], preferred_element_type=F32)
        core_copies[j].wait_recv()
        both = own + core_recv[j].astype(F32)
        part[j] = both
        x_send[j] = both.astype(BF16)
        for d in range(3):
            x_copies.append(
                start(
                    copy_to(
                        x_send.at[j, :, aligned(x_peers[d], 256)], x_recv.at[j, d],
                        x_ss.at[j, d], x_rs.at[j, d], at(z, y, x_peers[d], c),
                    )
                )
            )

    weights_step(1)

    rs_y = {}
    for j in range(CHUNKS):
        total = part[j, :, aligned(x, 256)]
        for d in range(3):
            x_copies[3 * j + d].wait_recv()
            total = total + x_recv[j, d].astype(F32)
        x_sum[j] = total
        y_send[j] = total.astype(BF16)
        for d in range(8):
            if d == 0 and j >= 2:
                continue
            yy = lax.rem(y + d, 8)
            rs_y[j, d] = start(
                copy_to(
                    y_send.at[j, aligned(yy, 16)], y_recv.at[j, d],
                    y_ss.at[j, d], y_rs.at[j, d], at(1 - z if j < 2 else z, yy, x, c),
                )
            )
        weights_step(j + 2)

    table = hadamard_table()
    signs = sign_table(c * 4096 + x * 1024 + z * 512)
    for copy in state_copies:
        copy.wait_recv()
    master, adam_m, adam_v, anchor, outer_mom = (
        jnp.concatenate(
            [state_in[pl.ds(4 * a + b, 16, stride=ARRAYS), :] for b in range(4)], axis=0
        )
        for a in range(5)
    )
    sums = []
    for k in range(2):
        total = x_sum[2 + k, aligned(y, 16), :]
        for j in (k, 2 + k):
            for d in range(8):
                if (j, d) in rs_y:
                    rs_y[j, d].wait_recv()
                    total = total + y_recv[j, d].astype(F32)
        sums += [total[:, :128], total[:, 128:]]
    gradient = jnp.concatenate(sums, axis=0)

    first = BETA_ONE * adam_m + (1.0 - BETA_ONE) * gradient
    second = BETA_TWO * adam_v + (1.0 - BETA_TWO) * gradient * gradient
    corr_one = 1.0 - BETA_ONE**STEP
    corr_two = 1.0 - BETA_TWO**STEP
    update = first / corr_one / (jnp.sqrt(second / corr_two) + EPS) + DECAY * master
    inner = master - INNER_LR * update
    rot[rep] = rotate((anchor - inner) * signs, table).astype(BF16)
    rep_copies = []
    for d in range(3):
        rep_copies.append(
            start(
                copy_to(
                    rot.at[rep], rot.at[rep], rep_ss.at[d], rep_rs.at[d],
                    {"rep": lax.rem(rep + d + 1, 4)},
                )
            )
        )
    for copy in nh_copies:
        copy.wait_recv()
    ahead = lax.dot_general(
        next_all[...], order, (((1,), (1,)), ((), ())), preferred_element_type=F32
    ).astype(BF16)
    for copy in rep_copies:
        copy.wait_recv()
    total = rot[0].astype(F32)
    for r in range(1, 4):
        total = total + rot[r].astype(F32)
    mean_delta = rotate(total, table) * signs * 0.25
    new_momentum = MOMENTUM * outer_mom + mean_delta
    new_anchor = anchor - OUTER_LR * (MOMENTUM * new_momentum + mean_delta)
    merged = ALPHA * inner + (1.0 - ALPHA) * new_anchor
    rows = aligned(y, 16)
    for b in range(4):
        gathered[rows, b * 128 : (b + 1) * 128] = merged[16 * b : 16 * b + 16].astype(BF16)
    agy_copies, stores = [], []
    for q in range(PARTS):
        view = gathered.at[rows, pl.ds(q * WIDE, WIDE)]
        for d in range(7):
            agy_copies.append(
                start(
                    copy_to(
                        view, view, agy_ss.at[q, d], agy_rs.at[q, d], at(z, y_peers[d], x, c)
                    )
                )
            )

    for a, value in enumerate((merged, new_anchor, new_momentum, jnp.zeros((64, 128), F32))):
        for b in range(4):
            back_send[pl.ds(4 * a + b, 16, stride=16), :] = value[16 * b : 16 * b + 16]
    back_copies = []
    for i, (zz, xx, cc) in enumerate(group):
        back_copies.append(
            start(
                copy_to(
                    back_send.at[aligned(zz * 8 + xx * 2 + cc, 16)],
                    back_recv.at[aligned(slice_here, 16)],
                    back_ss.at[i], back_rs.at[i], at(zz, y, xx, cc),
                )
            )
        )
    back_recv[aligned(slice_here, 16), :] = back_send[aligned(place, 16), :]

    def times_weights(h):
        products = jnp.zeros((256, 128), F32)
        for j in range(CHUNKS):
            for s in range(4):
                products = products + lax.dot_general(
                    cotv[h, j, :, s * 256 : (s + 1) * 256],
                    weights[h, :, aligned(s * 4 + lax.div(chunk_at[j], 256), 256)],
                    (((1,), (1,)), ((), ())), preferred_element_type=F32,
                )
        return products

    products = times_weights(1)

    last = []
    for q in range(PARTS):
        for d in range(7):
            agy_copies[7 * q + d].wait_recv()
        ahead_send[q] = jnp.dot(
            ahead, gathered[:, q * WIDE : (q + 1) * WIDE], preferred_element_type=F32
        ).astype(BF16)
        for i, (zz, xx, cc) in enumerate(group):
            last.append(
                start(
                    copy_to(
                        ahead_send.at[q, aligned(zz * 8 + xx * 2 + cc, 32)],
                        ahead_out.at[slice_here, q],
                        last_ss.at[q, i], last_rs.at[q, i], at(zz, y, xx, cc),
                    )
                )
            )

    for copy in agc_copies:
        copy.wait_recv()
    products = products + times_weights(0)
    grad_hidden[...] = jnp.dot(
        products.astype(BF16), order, preferred_element_type=F32
    ).astype(BF16)
    store = pltpu.make_async_copy(grad_hidden, grad_hidden_out, out_sem.at[3])
    store.start()
    stores.append(store)

    for copy in back_copies:
        copy.wait_recv()
    for a, out in enumerate((merged_out, anchor_out, mom_out)):
        for i in range(16):
            results[a, 4 * i : 4 * i + 4, :] = back_recv[16 * i + 4 * a : 16 * i + 4 * a + 4, :]
        store = pltpu.make_async_copy(results.at[a], out, out_sem.at[a])
        store.start()
        stores.append(store)

    sources = [slice_here]
    for dz in range(2):
        for dx in range(4):
            for dc in range(2):
                if dz or dx or dc:
                    sources.append(
                        (1 - c if dc else c) * 8
                        + lax.rem(x + 4 - dx, 4) * 2
                        + (1 - z if dz else z)
                    )
    for q in range(PARTS):
        for i, piece in enumerate(sources):
            view = ahead_send.at[q, seat]
            if i:
                last[15 * q + i - 1].wait_recv()
                view = ahead_out.at[piece, q]
            begin = pl.multiple_of(piece * 512 + q * WIDE, WIDE)
            store = pltpu.make_async_copy(
                view, next_out.at[:, pl.ds(begin, WIDE)], next_sem.at[q, i]
            )
            store.start()
            stores.append(store)
    for store in stores:
        store.wait()
    for copy in sends:
        copy.wait_send()


def store_kernel(*refs):
    sources, outs, held, sems = refs[:5], refs[5:10], refs[10:15], refs[15]
    inward = [pltpu.make_async_copy(a, b, sems.at[0, i]) for i, (a, b) in enumerate(zip(sources, held))]
    outward = [pltpu.make_async_copy(a, b, sems.at[1, i]) for i, (a, b) in enumerate(zip(held, outs))]
    for copy in inward:
        copy.start()
    for come, go in zip(inward, outward):
        come.wait()
        go.start()
    for copy in outward:
        copy.wait()


def shards(hidden, cotangent, master, adam_m, adam_v, anchor, outer_mom, next_hidden):
    hbm = pl.BlockSpec(memory_space=pltpu.HBM)
    dma = lambda *shape: pltpu.SemaphoreType.DMA(shape)
    row = lambda a: a.reshape(64, 128)
    shapes = (
        jax.ShapeDtypeStruct((256, 128), BF16),
        jax.ShapeDtypeStruct((64, 128), F32),
        jax.ShapeDtypeStruct((64, 128), F32),
        jax.ShapeDtypeStruct((64, 128), F32),
        jax.ShapeDtypeStruct((32, 8192), BF16),
    )
    outs = pl.pallas_call(
        kernel,
        out_shape=shapes,
        in_specs=[hbm] * 8,
        out_specs=(hbm,) * 5,
        scratch_shapes=[
            pltpu.VMEM((256, 128), BF16),
            pltpu.VMEM((3, 64, 128), F32),
            pltpu.VMEM((256, 128), BF16),
            pltpu.VMEM((5, 64, 128), F32),
            pltpu.VMEM((512, 128), BF16),
            pltpu.VMEM((2, CHUNKS, 256, 1024), BF16),
            pltpu.VMEM((CHUNKS, 128, 1024), BF16),
            pltpu.VMEM((CHUNKS, 128, 1024), BF16),
            pltpu.VMEM((CHUNKS, 128, 1024), F32),
            pltpu.VMEM((CHUNKS, 128, 1024), BF16),
            pltpu.VMEM((CHUNKS, 3, 128, 256), BF16),
            pltpu.VMEM((CHUNKS, 128, 256), F32),
            pltpu.VMEM((CHUNKS, 128, 256), BF16),
            pltpu.VMEM((CHUNKS, 8, 16, 256), BF16),
            pltpu.VMEM((16 * ARRAYS, 128), F32),
            pltpu.VMEM((16 * ARRAYS, 128), F32),
            pltpu.VMEM((4, 64, 128), BF16),
            pltpu.VMEM((64, 128), BF16),
            pltpu.VMEM((16, 32, 128), BF16),
            pltpu.VMEM((512, 128), F32),
            pltpu.VMEM((128, 512), BF16),
            pltpu.VMEM((256, 128), F32),
            pltpu.VMEM((256, 128), F32),
            pltpu.VMEM((2, 128, 4096), BF16),
            pltpu.VMEM((PARTS, 512, WIDE), BF16),
            pltpu.VMEM((16, PARTS, 32, WIDE), BF16),
            dma(4), dma(PARTS, 16), dma(3), dma(4), dma(2, CHUNKS, 4), dma(15), dma(15),
            dma(CHUNKS), dma(CHUNKS), dma(CHUNKS, 3), dma(CHUNKS, 3),
            dma(CHUNKS, 8), dma(CHUNKS, 8), dma(15), dma(15), dma(3), dma(3),
            dma(15), dma(15), dma(PARTS, 7), dma(PARTS, 7), dma(15), dma(15),
            dma(2, 4), dma(2, 4), dma(8), dma(8), dma(PARTS, 15), dma(PARTS, 15),
        ],
        compiler_params=pltpu.CompilerParams(
            collective_id=0, has_side_effects=True, vmem_limit_bytes=VMEM_BYTES
        ),
        name="sync",
    )(
        hidden[0], cotangent[0], row(master), row(adam_m), row(adam_v),
        row(anchor), row(outer_mom), next_hidden[0],
    )
    outs = pl.pallas_call(
        store_kernel,
        out_shape=shapes,
        in_specs=[hbm] * 5,
        out_specs=(hbm,) * 5,
        scratch_shapes=[pltpu.VMEM(s.shape, s.dtype) for s in shapes] + [dma(2, 5)],
        compiler_params=pltpu.CompilerParams(vmem_limit_bytes=VMEM_BYTES),
        name="store",
    )(*outs)
    grad_hidden, merged, new_anchor, new_momentum, next_out = outs
    return (
        grad_hidden[None],
        merged.reshape(1, 1, 8192),
        new_anchor.reshape(1, 8192),
        new_momentum.reshape(1, 8192),
        next_out[None],
    )


def solution(mesh):
    in_specs = (
        P("rep", "fsdp", None),
        P("rep", "fsdp", None),
        P("rep", "fsdp", None),
        P("rep", "fsdp", None),
        P("rep", "fsdp", None),
        P("fsdp", None),
        P("fsdp", None),
        P("rep", "fsdp", None),
    )
    out_specs = (
        P("rep", "fsdp", None),
        P("rep", "fsdp", None),
        P("fsdp", None),
        P("fsdp", None),
        P("rep", "fsdp", None),
    )
    return jax.shard_map(shards, mesh=mesh, in_specs=in_specs, out_specs=out_specs, check_vma=False)
```

time: 86 us -> 68.1 us (0.79)
  Pallas kernels: 85.2 us -> 67.3 us
    pallas_call x1, Pallas kernels: 83.1 us -> 65.3 us  [shards(): pl.pallas_call(kernel, out_shape=shapes, in_specs=[hbm] * 8, out_specs=(h...]
where the time goes in v3:
time: 68.1 us; the launch traced here: 67.9 us
  Pallas kernels  67.3 us (99%)
    pallas_call x1, Pallas kernels, shards(): pl.pallas_call(kernel, out_shape=shapes, in_specs=[hbm] * 8, out_specs=(h...  65.3 us
    pallas_call x1, Pallas kernels, shards(): pl.pallas_call(store_kernel, out_shape=shapes, in_specs=[hbm] * 5, out_sp...  2.02 us

profile of v3, /device:TPU:1, one launch (start us, length us, event | category | flops | bytes accessed | tf_op | source)
XLA Modules:
  0.0 67.9 jit_solution(18128610578346330730)
XLA Ops:
  0.6 65.3 %sync.1 = (bf16[256,128]{1,0:T(8,128)(2,1)}, f32[64,128]{1,0:T(8,128)}, f32[64,128]{1,0:T(8,128)}, f32[64,128]{1,0:T(8,128)}, bf16[32,8192]{1,0:T(8,128)(2,1)}) custom-call(bf16[256,128]{1,0:T(8,128)(2,1)} %bitcast.14, bf16[256,8192]{1,0:T(8,128)(2,1)} %bitcast.13, f32[64,128]{1,0:T(8,128)} %bitcast.15, f32[64,128]{1,0:T(8,128)} %bitcast.16, ...), custom_call_target="tpu_custom_call" | custom-call | tf_op jit(solution)/shard_map/sync/pallas_call | solution.py:494
  65.9 2.0 %store.1 = (bf16[256,128]{1,0:T(8,128)(2,1)}, f32[64,128]{1,0:T(8,128)}, f32[64,128]{1,0:T(8,128)}, f32[64,128]{1,0:T(8,128)}, bf16[32,8192]{1,0:T(8,128)(2,1)}) custom-call(bf16[256,128]{1,0:T(8,128)(2,1)} %get-tuple-element.15.refs_0_, f32[64,128]{1,0:T(8,128)} %get-tuple-element.16.refs_1_, f32[64,128]{1,0:T(8,128)} %get-tuple-element.17.refs_2_, ...), custom_call_target="tpu_custom_call" | custom-call | tf_op jit(solution)/shard_map/store/pallas_call | solution.py:540

commit v4 on v3

--- a/solution.py
+++ b/solution.py
@@ -136,8 +136,8 @@
         load.start()
     chunk_at = [(1 - z if j < 2 else z) * 512 + j % 2 * 256 for j in range(CHUNKS)]
     cot_loads = {}
-    for h in range(2):
-        for j in range(CHUNKS):
+    for j in range(CHUNKS):
+        for h in range(2):
             for s in range(4):
                 begin = pl.multiple_of(halves[h] * 4096 + s * 1024 + chunk_at[j], 256)
                 load = pltpu.make_async_copy(
@@ -222,51 +222,9 @@
             to_partner(step - 1)
 
     core_copies = []
-    for j in range(CHUNKS):
-        for s in range(4):
-            cot_loads[0, j, s].wait()
-        core_send[j] = jnp.dot(turned, cotv[0, j], preferred_element_type=F32).astype(BF16)
-        if j == 0:
-            pl.semaphore_wait(barrier, len(peers))
-        core_copies.append(
-            start(
-                copy_to(
-                    core_send.at[j], core_recv.at[j], core_ss.at[j], core_rs.at[j], partner
-                )
-            )
-        )
-    weights_start()
-
-    for load in late_loads:
-        load.wait()
-    for i in range(16):
-        for a in range(5):
-            packed[i * ARRAYS + 4 * a : i * ARRAYS + 4 * a + 4, :] = state[a, 4 * i : 4 * i + 4, :]
-        packed[i * ARRAYS + 20 : i * ARRAYS + 24, :] = jnp.zeros((4, 128), F32)
-    state_copies, nh_copies = [], []
-    loads[2].wait()
-    for i, (zz, xx, cc) in enumerate(group):
-        state_copies.append(
-            start(
-                copy_to(
-                    packed.at[aligned(cc * 8 + xx * 2 + zz, ARRAYS)],
-                    state_in.at[aligned(place, ARRAYS)],
-                    st_ss.at[i], st_rs.at[i], at(zz, y, xx, cc),
-                )
-            )
-        )
-        nh_copies.append(
-            start(
-                copy_to(
-                    next_all.at[seat], next_all.at[seat],
-                    nh_ss.at[i], nh_rs.at[i], at(zz, y, xx, cc),
-                )
-            )
-        )
-    state_in[aligned(place, ARRAYS), :] = packed[aligned(slice_here, ARRAYS), :]
-
     x_copies = []
-    for j in range(CHUNKS):
+
+    def chunk_to_x(j):
         for s in range(4):
             cot_loads[1, j, s].wait()
         own = jnp.dot(turned, cotv[1, j], preferred_element_type=F32)
@@ -284,7 +242,43 @@
                 )
             )
 
+    for j in range(CHUNKS):
+        for s in range(4):
+            cot_loads[0, j, s].wait()
+        core_send[j] = jnp.dot(turned, cotv[0, j], preferred_element_type=F32).astype(BF16)
+        if j == 0:
+            pl.semaphore_wait(barrier, len(peers))
+            weights_start()
+        core_copies.append(
+            start(
+                copy_to(
+                    core_send.at[j], core_recv.at[j], core_ss.at[j], core_rs.at[j], partner
+                )
+            )
+        )
+        if j:
+            chunk_to_x(j - 1)
+    chunk_to_x(CHUNKS - 1)
     weights_step(1)
+
+    for load in late_loads:
+        load.wait()
+    for i in range(16):
+        for a in range(5):
+            packed[i * ARRAYS + 4 * a : i * ARRAYS + 4 * a + 4, :] = state[a, 4 * i : 4 * i + 4, :]
+        packed[i * ARRAYS + 20 : i * ARRAYS + 24, :] = jnp.zeros((4, 128), F32)
+    state_copies = []
+    for i, (zz, xx, cc) in enumerate(group):
+        state_copies.append(
+            start(
+                copy_to(
+                    packed.at[aligned(cc * 8 + xx * 2 + zz, ARRAYS)],
+                    state_in.at[aligned(place, ARRAYS)],
+                    st_ss.at[i], st_rs.at[i], at(zz, y, xx, cc),
+                )
+            )
+        )
+    state_in[aligned(place, ARRAYS), :] = packed[aligned(slice_here, ARRAYS), :]
 
     rs_y = {}
     for j in range(CHUNKS):
@@ -304,7 +298,8 @@
                     y_ss.at[j, d], y_rs.at[j, d], at(1 - z if j < 2 else z, yy, x, c),
                 )
             )
-        weights_step(j + 2)
+        if j == 0:
+            weights_step(2)
 
     table = hadamard_table()
     signs = sign_table(c * 4096 + x * 1024 + z * 512)
@@ -344,11 +339,18 @@
                 )
             )
         )
-    for copy in nh_copies:
-        copy.wait_recv()
-    ahead = lax.dot_general(
-        next_all[...], order, (((1,), (1,)), ((), ())), preferred_element_type=F32
-    ).astype(BF16)
+    weights_step(3)
+    loads[2].wait()
+    nh_copies = []
+    for i, (zz, xx, cc) in enumerate(group):
+        nh_copies.append(
+            start(
+                copy_to(
+                    next_all.at[seat], next_all.at[seat],
+                    nh_ss.at[i], nh_rs.at[i], at(zz, y, xx, cc),
+                )
+            )
+        )
     for copy in rep_copies:
         copy.wait_recv()
     total = rot[0].astype(F32)
@@ -400,7 +402,12 @@
                 )
         return products
 
-    products = times_weights(1)
+    for copy in nh_copies:
+        copy.wait_recv()
+    ahead = lax.dot_general(
+        next_all[...], order, (((1,), (1,)), ((), ())), preferred_element_type=F32
+    ).astype(BF16)
+    weights_step(4)
 
     last = []
     for q in range(PARTS):
@@ -420,6 +427,8 @@
                 )
             )
 
+    weights_step(5)
+    products = times_weights(1)
     for copy in agc_copies:
         copy.wait_recv()
     products = products + times_weights(0)

time: 68.1 us -> 62.5 us (0.918)
  Pallas kernels: 67.3 us -> 61.7 us
    pallas_call x1, Pallas kernels: 65.3 us -> 59.7 us  [shards(): pl.pallas_call(kernel, out_shape=shapes, in_specs=[hbm] * 8, out_specs=(h...]
where the time goes in v4:
time: 62.5 us; the launch traced here: 62.3 us
  Pallas kernels  61.7 us (99%)
  between operations  0.64 us (1%)
    pallas_call x1, Pallas kernels, shards(): pl.pallas_call(kernel, out_shape=shapes, in_specs=[hbm] * 8, out_specs=(h...  59.7 us
    pallas_call x1, Pallas kernels, shards(): pl.pallas_call(store_kernel, out_shape=shapes, in_specs=[hbm] * 5, out_sp...  2.02 us

profile of v4, /device:TPU:1, one launch (start us, length us, event | category | flops | bytes accessed | tf_op | source)
XLA Modules:
  0.0 62.3 jit_solution(5347486274926805945)
XLA Ops:
  0.6 59.7 %sync.1 = (bf16[256,128]{1,0:T(8,128)(2,1)}, f32[64,128]{1,0:T(8,128)}, f32[64,128]{1,0:T(8,128)}, f32[64,128]{1,0:T(8,128)}, bf16[32,8192]{1,0:T(8,128)(2,1)}) custom-call(bf16[256,128]{1,0:T(8,128)(2,1)} %bitcast.14, bf16[256,8192]{1,0:T(8,128)(2,1)} %bitcast.13, f32[64,128]{1,0:T(8,128)} %bitcast.15, f32[64,128]{1,0:T(8,128)} %bitcast.16, ...), custom_call_target="tpu_custom_call" | custom-call | tf_op jit(solution)/shard_map/sync/pallas_call | solution.py:503
  60.3 2.0 %store.1 = (bf16[256,128]{1,0:T(8,128)(2,1)}, f32[64,128]{1,0:T(8,128)}, f32[64,128]{1,0:T(8,128)}, f32[64,128]{1,0:T(8,128)}, bf16[32,8192]{1,0:T(8,128)(2,1)}) custom-call(bf16[256,128]{1,0:T(8,128)(2,1)} %get-tuple-element.15.refs_0_, f32[64,128]{1,0:T(8,128)} %get-tuple-element.16.refs_1_, f32[64,128]{1,0:T(8,128)} %get-tuple-element.17.refs_2_, ...), custom_call_target="tpu_custom_call" | custom-call | tf_op jit(solution)/shard_map/store/pallas_call | solution.py:549

commit v5 on v4

--- a/solution.py
+++ b/solution.py
@@ -23,6 +23,12 @@
 CHUNKS = 4
 PARTS = 2
 WIDE = 512 // PARTS
+OFFSETS = sorted(
+    ((dz, dx, dc) for dz in range(2) for dx in range(4) for dc in range(2) if dz or dx or dc),
+    key=lambda offset: -(offset[0] + min(offset[1], 4 - offset[1])),
+)
+FAR_Y = (4, 3, 5, 2, 6, 1, 7)
+FAR_X = (1, 0, 2)
 ARRAYS = 24
 
 
@@ -93,14 +99,9 @@
     def at(zz, yy, xx, cc):
         return {"fsdp": zz * 64 + yy * 8 + xx * 2 + cc}
 
-    group = []
-    for dz in range(2):
-        for dx in range(4):
-            for dc in range(2):
-                if dz or dx or dc:
-                    group.append(
-                        (1 - z if dz else z, lax.rem(x + dx, 4), 1 - c if dc else c)
-                    )
+    group = [
+        (1 - z if dz else z, lax.rem(x + dx, 4), 1 - c if dc else c) for dz, dx, dc in OFFSETS
+    ]
     place = z * 8 + x * 2 + c
     slice_here = c * 8 + x * 2 + z
     partner = at(z, y, x, 1 - c)
@@ -222,7 +223,7 @@
             to_partner(step - 1)
 
     core_copies = []
-    x_copies = []
+    x_copies = {}
 
     def chunk_to_x(j):
         for s in range(4):
@@ -232,13 +233,11 @@
         both = own + core_recv[j].astype(F32)
         part[j] = both
         x_send[j] = both.astype(BF16)
-        for d in range(3):
-            x_copies.append(
-                start(
-                    copy_to(
-                        x_send.at[j, :, aligned(x_peers[d], 256)], x_recv.at[j, d],
-                        x_ss.at[j, d], x_rs.at[j, d], at(z, y, x_peers[d], c),
-                    )
+        for d in FAR_X:
+            x_copies[j, d] = start(
+                copy_to(
+                    x_send.at[j, :, aligned(x_peers[d], 256)], x_recv.at[j, d],
+                    x_ss.at[j, d], x_rs.at[j, d], at(z, y, x_peers[d], c),
                 )
             )
 
@@ -284,11 +283,11 @@
     for j in range(CHUNKS):
         total = part[j, :, aligned(x, 256)]
         for d in range(3):
-            x_copies[3 * j + d].wait_recv()
+            x_copies[j, d].wait_recv()
             total = total + x_recv[j, d].astype(F32)
         x_sum[j] = total
         y_send[j] = total.astype(BF16)
-        for d in range(8):
+        for d in FAR_Y + (0,):
             if d == 0 and j >= 2:
                 continue
             yy = lax.rem(y + d, 8)
@@ -330,7 +329,7 @@
     inner = master - INNER_LR * update
     rot[rep] = rotate((anchor - inner) * signs, table).astype(BF16)
     rep_copies = []
-    for d in range(3):
+    for d in FAR_X:
         rep_copies.append(
             start(
                 copy_to(
@@ -366,7 +365,7 @@
     agy_copies, stores = [], []
     for q in range(PARTS):
         view = gathered.at[rows, pl.ds(q * WIDE, WIDE)]
-        for d in range(7):
+        for d in (far - 1 for far in FAR_Y):
             agy_copies.append(
                 start(
                     copy_to(
@@ -449,15 +448,10 @@
         stores.append(store)
 
     sources = [slice_here]
-    for dz in range(2):
-        for dx in range(4):
-            for dc in range(2):
-                if dz or dx or dc:
-                    sources.append(
-                        (1 - c if dc else c) * 8
-                        + lax.rem(x + 4 - dx, 4) * 2
-                        + (1 - z if dz else z)
-                    )
+    for dz, dx, dc in OFFSETS:
+        sources.append(
+            (1 - c if dc else c) * 8 + lax.rem(x + 4 - dx, 4) * 2 + (1 - z if dz else z)
+        )
     for q in range(PARTS):
         for i, piece in enumerate(sources):
             view = ahead_send.at[q, seat]

time: 62.5 us -> 60.9 us (0.974)
  Pallas kernels: 61.7 us -> 60.1 us
    pallas_call x1, Pallas kernels: 59.7 us -> 58.1 us  [shards(): pl.pallas_call(kernel, out_shape=shapes, in_specs=[hbm] * 8, out_specs=(h...]
where the time goes in v5:
time: 60.9 us; the launch traced here: 60.8 us
  Pallas kernels  60.1 us (99%)
  between operations  0.64 us (1%)
    pallas_call x1, Pallas kernels, shards(): pl.pallas_call(kernel, out_shape=shapes, in_specs=[hbm] * 8, out_specs=(h...  58.1 us
    pallas_call x1, Pallas kernels, shards(): pl.pallas_call(store_kernel, out_shape=shapes, in_specs=[hbm] * 5, out_sp...  2.02 us

profile of v5, /device:TPU:1, one launch (start us, length us, event | category | flops | bytes accessed | tf_op | source)
XLA Modules:
  0.0 60.8 jit_solution(4472550834484563689)
XLA Ops:
  0.6 58.1 %sync.1 = (bf16[256,128]{1,0:T(8,128)(2,1)}, f32[64,128]{1,0:T(8,128)}, f32[64,128]{1,0:T(8,128)}, f32[64,128]{1,0:T(8,128)}, bf16[32,8192]{1,0:T(8,128)(2,1)}) custom-call(bf16[256,128]{1,0:T(8,128)(2,1)} %bitcast.14, bf16[256,8192]{1,0:T(8,128)(2,1)} %bitcast.13, f32[64,128]{1,0:T(8,128)} %bitcast.15, f32[64,128]{1,0:T(8,128)} %bitcast.16, ...), custom_call_target="tpu_custom_call" | custom-call | tf_op jit(solution)/shard_map/sync/pallas_call | solution.py:497
  58.8 2.0 %store.1 = (bf16[256,128]{1,0:T(8,128)(2,1)}, f32[64,128]{1,0:T(8,128)}, f32[64,128]{1,0:T(8,128)}, f32[64,128]{1,0:T(8,128)}, bf16[32,8192]{1,0:T(8,128)(2,1)}) custom-call(bf16[256,128]{1,0:T(8,128)(2,1)} %get-tuple-element.15.refs_0_, f32[64,128]{1,0:T(8,128)} %get-tuple-element.16.refs_1_, f32[64,128]{1,0:T(8,128)} %get-tuple-element.17.refs_2_, ...), custom_call_target="tpu_custom_call" | custom-call | tf_op jit(solution)/shard_map/store/pallas_call | solution.py:543
